TPU v7x, 32 devices: a whole 2x2x4 slice. The times are simulated.
32 devices in a mesh: dp: 8 (over z, x), tensor: 4 (over y, core).
Axes of the slice: x: 2, y: 2, z: 4, core: 2. Of those that a mesh axis runs over, the one named last changes fastest.
Arguments:
- query_states: bfloat16 [1, 8192, 1024], P(None, 'dp', 'tensor'), may hold values from -6 to 6
- key_states: bfloat16 [1, 8192, 1024], P(None, 'dp', 'tensor'), may hold values from -6 to 6
- value_states: bfloat16 [1, 8192, 1024], P(None, 'dp', 'tensor'), may hold values from -6 to 6
- joining_weight: bfloat16 [1, 1024, 2048], P(None, 'tensor'), may hold values from -0.1875 to 0.1875
- norm_gain: float32 [2048], replicated, may hold values from 0.1 to 1.9
- next_hidden: bfloat16 [8192, 2048], P(('dp', 'tensor')), may hold values from -6 to 6
- lengths: int32 [8], P('dp'), may hold values from 256 to 1024
- vote_counts: int32 [8], P('dp'), may hold values from 1 to 8
Outputs:
- draft_hidden: bfloat16 [8192, 2048], P(('dp', 'tensor'))
- weight_grad: bfloat16 [1, 1024, 2048], P(None, 'tensor', 'dp')
- gain_grad: float32 [2048], replicated
- draft_loss: float32 [], replicated
All inputs are finite; a program needn't handle non-finite values.
Results may differ from a plain program's by a relative error of at most 0.014.
Values may be sent and summed in bfloat16 or wider, within the bound.
No kernel may reach another device: no remote copies, remote signals or barrier semaphores. Data moves between devices by JAX's collectives and lax.ppermute only.
A program may use at most 64 MiB of HBM per device.

v0:
```python
import math
import jax
import jax.numpy as jnp
from jax import lax
from jax.sharding import PartitionSpec as P

HD = 128
loss_scale = 65536.0
neg_large = -1e30


def on_device(
    query_states,
    key_states,
    value_states,
    joining_weight,
    norm_gain,
    next_hidden,
    lengths,
    vote_counts,
):
    n_layers, tok_group, col_width = query_states.shape
    chains = lengths.shape[0]
    seq_len = tok_group // chains
    heads_here = col_width // HD
    shaped = (n_layers, chains, seq_len, heads_here, HD)
    scores = jnp.einsum(
        "lcqhd,lckhd->lchqk",
        query_states.reshape(shaped),
        key_states.reshape(shaped),
        preferred_element_type=jnp.float32,
    ) / math.sqrt(HD)
    positions = jnp.arange(seq_len)
    causal = positions[None, :] <= positions[:, None]
    key_valid = positions[None, :] < lengths[:, None]
    visible = causal[None, None, None, :, :] & key_valid[None, :, None, None, :]
    scores = jnp.where(visible, scores, neg_large)
    row_peak = jnp.max(scores, axis=-1, keepdims=True)
    exponent = jnp.exp(scores - row_peak)
    attn_probs = (exponent / jnp.sum(exponent, axis=-1, keepdims=True)).astype(jnp.bfloat16)
    context = jnp.einsum(
        "lchqk,lckhd->lcqhd",
        attn_probs,
        value_states.reshape(shaped),
        preferred_element_type=jnp.float32,
    )
    context = context.astype(jnp.bfloat16).reshape(n_layers, tok_group, col_width)
    own_rows = next_hidden.shape[0]
    offset = lax.axis_index("tensor") * own_rows
    partial_sum = jnp.einsum(
        "ltc,lcd->td", context, joining_weight, preferred_element_type=jnp.float32
    )
    summed = lax.psum(partial_sum.astype(jnp.bfloat16), "tensor").astype(jnp.float32)
    joined_rows = lax.dynamic_slice_in_dim(summed, offset, own_rows, 0)
    token_pos = offset + jnp.arange(own_rows, dtype=jnp.int32)
    chain_of = token_pos // seq_len
    in_chain = token_pos % seq_len
    onehot = (chain_of[:, None] == jnp.arange(chains)[None, :]).astype(jnp.float32)
    tok_votes = jnp.dot(onehot, vote_counts.astype(jnp.float32), precision=lax.Precision.HIGHEST)
    tok_length = jnp.dot(onehot, lengths.astype(jnp.float32), precision=lax.Precision.HIGHEST)
    token_weight = jnp.where(in_chain.astype(jnp.float32) < tok_length - 1.0, tok_votes, 0.0)
    inv_rms = lax.rsqrt(jnp.mean(joined_rows * joined_rows, axis=-1, keepdims=True) + 1e-06)
    normed = joined_rows * inv_rms
    predicted = normed * norm_gain
    draft_hidden = predicted.astype(jnp.bfloat16)
    misfit = predicted - next_hidden.astype(jnp.float32)
    local_loss = jnp.sum(token_weight * jnp.mean(misfit * misfit, axis=-1))
    grad_pred = loss_scale * 2.0 / joined_rows.shape[1] * token_weight[:, None] * misfit
    local_gain = jnp.sum(grad_pred * normed, axis=0)
    grad_normed = grad_pred * norm_gain
    grad_joined = (
        inv_rms * (grad_normed - normed * jnp.mean(grad_normed * normed, axis=-1, keepdims=True))
    ).astype(jnp.bfloat16)
    gain_sum, loss_sum, weight_total = lax.psum(
        (local_gain, local_loss, jnp.sum(token_weight)), ("dp", "tensor")
    )
    grad_total = jnp.einsum(
        "ltc,td->lcd",
        context,
        lax.all_gather(grad_joined, "tensor", axis=0, tiled=True),
        preferred_element_type=jnp.float32,
    )
    grad_cols = lax.psum_scatter(
        grad_total.astype(jnp.bfloat16), "dp", scatter_dimension=2, tiled=True
    ).astype(jnp.float32)
    weight_grad = (grad_cols / weight_total).astype(jnp.bfloat16)
    return (draft_hidden, weight_grad, gain_sum / weight_total, loss_sum / weight_total)


def solution(mesh):
    return jax.shard_map(
        on_device,
        mesh=mesh,
        in_specs=(
            P(None, "dp", "tensor"),
            P(None, "dp", "tensor"),
            P(None, "dp", "tensor"),
            P(None, "tensor", None),
            P(),
            P(("dp", "tensor"), None),
            P("dp"),
            P("dp"),
        ),
        out_specs=(P(("dp", "tensor"), None), P(None, "tensor", "dp"), P(), P()),
        check_vma=False,
    )
```

profile of v0, /device:TPU:0, one launch (start us, length us, event | category | flops | bytes accessed | tf_op | source)
XLA Modules:
  0.0 236.3 jit_solution(4800602347688197091)
XLA Ops:
  7.2 0.0 copy-start
  7.2 0.0 copy-start.2
  7.2 0.0 copy-start.3
  7.2 0.0 all-reduce.3.cloned.1.call-start
  8.0 0.4 fusion.4
  8.4 2.0 reshape.122
  10.4 0.0 copy-done.2
  10.4 1.0 reshape.123
  11.4 0.0 copy-done.3
  11.4 1.0 copy.17
  12.4 7.7 %fusion.39 = (f32[2,1024]{1,0:T(2,128)S(1)}, f32[2,1024,1024]{1,2,0:T(8,128)}) fusion(pred[1024,1024]{0,1:T(8,128)(4,1)S(1)} %fusion.4, bf16[1024,2,128]{2,1,0:T(2,128)(2,1)} %reshape.123, bf16[1024,2,128]{2,1,0:T(2,128)(2,1)} %reshape.122), kind=kOutput, calls=%fused_computation.54 | convolution fusion | flops 545260544 | bytes 10493952 | tf_op jit(solution)/shard_map/sub | solution.py:39
  20.1 0.0 copy-done.4
  20.1 4.1 %fusion.20 = bf16[2,1024,128]{1,2,0:T(8,128)(2,1)S(1)} fusion(bf16[1024,2,128]{0,2,1:T(8,128)(2,1)S(1)} %bitcast.23, f32[2,1024,1024]{1,2,0:T(8,128)} %get-tuple-element.13, f32[2,1024]{1,0:T(2,128)S(1)} %get-tuple-element.12), kind=kOutput, calls=%fused_computation.29 | convolution fusion | flops 541327360 | bytes 9445376 | tf_op jit(solution)/shard_map/lchqk,lckhd->lcqhd/dot_general | solution.py:41
  24.3 0.0 copy-done
  24.3 3.3 %convolution_convert_fusion = bf16[1024,2048]{1,0:T(8,128)(2,1)} fusion(bf16[1024,256]{0,1:T(8,128)(2,1)S(1)} %bitcast.21, bf16[1,256,2048]{2,1,0:T(8,128)(2,1)S(1)} %copy-done), kind=kOutput, calls=%fused_computation.11 | convolution fusion | flops 1075838976 | bytes 5767168 | tf_op jit(solution)/shard_map/ltc,lcd->td/dot_general | solution.py:50
  27.5 0.0 all-reduce.3.cloned.1.call-update
  27.6 0.0 all-gather.2.cloned.1.call-start
  28.3 0.6 broadcast_multiply_fusion
  29.0 86.9 %all-reduce.3.cloned.1.call-done = bf16[1024,2048]{1,0:T(8,128)(2,1)} async-done(((bf16[1024,2048]{1,0:T(8,128)(2,1)}), bf16[1024,2048]{1,0:T(8,128)(2,1)}) %all-reduce.3.cloned.1.call-update) | async-done | bytes 4194320 | tf_op jit(solution)/shard_map/psum | solution.py:53
  115.9 1.5 fusion.19
  117.4 2.3 fusion.18
  119.8 3.4 %fusion.17 = (bf16[256,2048]{1,0:T(8,128)(2,1)}, bf16[256,2048]{1,0:T(8,128)(2,1)}) fusion(bf16[256,2048]{1,0:T(8,128)(2,1)S(1)} %copy-done.1, f32[256]{0:T(256)S(1)} %broadcast_multiply_fusion.1, f32[256]{0:T(256)S(1)} %get-tuple-element.14, f32[2048]{0:T(1024)S(1)} %copy-done.5, f32[256]{0:T(256)S(1)} %add_rsqrt_fusion, ...), kind=kLoop, calls=%fused_computation.25 | loop fusion | flops 6291456 | bytes 4205572 | tf_op jit(solution)/shard_map/convert_element_type | solution.py:73
  123.2 0.0 all-gather.2.cloned.1.call-update
  123.2 0.0 reduce-scatter.2.cloned.1.call-start
  123.3 34.7 %all-gather.2.cloned.1.call-done = bf16[1024,2048]{1,0:T(8,128)(2,1)} async-done(((bf16[256,2048]{1,0:T(8,128)(2,1)}), bf16[1024,2048]{1,0:T(8,128)(2,1)}) %all-gather.2.cloned.1.call-update) | async-done | bytes 4194320 | tf_op jit(solution)/shard_map/all_gather | solution.py:80
  158.0 4.4 %fusion.11 = bf16[1,256,2048]{2,1,0:T(8,128)(2,1)} fusion(bf16[1024,256]{0,1:T(8,128)(2,1)S(1)} %bitcast.22, bf16[1024,2048]{1,0:T(8,128)(2,1)} %all-gather.2.cloned.1.call-done), kind=kOutput, calls=%fused_computation.19 | convolution fusion | flops 1074266112 | bytes 5767168 | tf_op jit(solution)/shard_map/ltc,td->lcd/dot_general | solution.py:77
  162.4 0.0 reduce-scatter.2.cloned.1.call-update
  162.4 0.7 multiply_reduce_fusion.1
  163.1 39.7 %all-reduce = (f32[]{:T(128)}, f32[2048]{0:T(1024)S(1)}, f32[]{:T(128)}) all-reduce(f32[]{:T(128)} %get-tuple-element.15, f32[2048]{0:T(1024)S(1)} %get-tuple-element.4, f32[]{:T(128)} %multiply_reduce_fusion.1), channel_id=1, replica_groups=mesh['dp'=8,'tensor'=4] {'dp','tensor'}, use_global_device_ids=true, to_apply=%region_7.8 | all-reduce | flops 2050 | bytes 16400 | tf_op jit(solution)/shard_map/psum | solution.py:74
  204.1 1.2 broadcast_divide_fusion
  205.2 21.3 %reduce-scatter.2.cloned.1.call-done = bf16[1,256,256]{2,1,0:T(8,128)(2,1)} async-done(((bf16[1,256,2048]{2,1,0:T(8,128)(2,1)}), bf16[1,256,256]{2,1,0:T(8,128)(2,1)}) %reduce-scatter.2.cloned.1.call-update) | async-done | bytes 131088 | tf_op jit(solution)/shard_map/reduce_scatter | solution.py:83
  226.5 2.1 divide_convert_fusion.4
  (8 shorter events, 0.0 us)
Async XLA Ops:
  7.2 17.1 %copy-start = (bf16[1,256,2048]{2,1,0:T(8,128)(2,1)S(1)}, bf16[1,256,2048]{2,1,0:T(8,128)(2,1)}, u32[]{:S(2)}) copy-start(bf16[1,256,2048]{2,1,0:T(8,128)(2,1)} %param.11) | copy-start | bytes 3145732
  7.2 3.3 %copy-start.2 = (bf16[1,1024,256]{2,1,0:T(8,128)(2,1)S(1)}, bf16[1,1024,256]{2,1,0:T(8,128)(2,1)}, u32[]{:S(2)}) copy-start(bf16[1,1024,256]{2,1,0:T(8,128)(2,1)} %param.9) | copy-start | bytes 1572868
  7.2 4.2 %copy-start.3 = (bf16[1,1024,256]{2,1,0:T(8,128)(2,1)S(1)}, bf16[1,1024,256]{2,1,0:T(8,128)(2,1)}, u32[]{:S(2)}) copy-start(bf16[1,1024,256]{2,1,0:T(8,128)(2,1)} %param.10) | copy-start | bytes 1572868
  7.2 108.7 %all-reduce.3.cloned.1.call-start = ((), (), s32[]{:S(2)}) async-start(), calls=%async_computation.1 | async-start | bytes 8388608 | tf_op jit(solution)/shard_map/psum | solution.py:53
  12.4 7.7 %copy-start.4 = (bf16[1,1024,256]{1,2,0:T(8,128)(2,1)S(1)}, bf16[1,1024,256]{1,2,0:T(8,128)(2,1)}, u32[]{:S(2)}) copy-start(bf16[1,1024,256]{1,2,0:T(8,128)(2,1)} %copy.17) | copy-start | bytes 1572868
  27.5 89.9 %copy-start.1 = (bf16[256,2048]{1,0:T(8,128)(2,1)S(1)}, bf16[256,2048]{1,0:T(8,128)(2,1)}, u32[]{:S(2)}) copy-start(bf16[256,2048]{1,0:T(8,128)(2,1)} %param.13) | copy-start | bytes 3145732
  27.5 89.9 %copy-start.5 = (f32[2048]{0:T(1024)S(1)}, f32[2048]{0:T(1024)}, u32[]{:S(2)}) copy-start(f32[2048]{0:T(1024)} %param.12) | copy-start | bytes 24580
  27.6 130.4 %all-gather.2.cloned.1.call-start = ((), (), s32[]{:S(2)}) async-start(), calls=%async_computation.2 | async-start | bytes 5242880 | tf_op jit(solution)/shard_map/all_gather | solution.py:80
  123.2 103.3 %reduce-scatter.2.cloned.1.call-start = ((), (), s32[]{:S(2)}) async-start(), calls=%async_computation.3 | async-start | bytes 1179648 | tf_op jit(solution)/shard_map/reduce_scatter | solution.py:83
Sparse Core Ops, SparseCore 0:
  27.7 88.1 all-reduce.2
  123.3 34.6 all-gather.1
  162.5 63.9 reduce-scatter.1
where the time goes:
time: 237 us; the launch traced here: 236 us
  waiting for transfers between devices  143 us (60%)
  blocking collectives  39.7 us (17%)
  matrix products  19.5 us (8%)
  between operations  17.7 us (7%)
  other arithmetic  12.2 us (5%)
  local copies, waits for them, and re-layouts  4.04 us (2%)
    psum x1, waiting for transfers between devices, on_device(): lax.psum(partial_sum.astype(jnp.bfloat16), 'tensor').astype(jnp.float32)  86.9 us
    psum x1, blocking collectives, on_device(): lax.psum((local_gain, local_loss, jnp.sum(token_weight)), ('dp', 'tensor'))  39.7 us
    all_gather x1, waiting for transfers between devices, on_device(): lax.all_gather(grad_joined, 'tensor', axis=0, tiled=True)  34.7 us
    reduce_scatter x1, waiting for transfers between devices, on_device(): lax.psum_scatter(grad_total.astype(jnp.bfloat16), 'dp', scatter_dimension...  21.3 us
    sub x1, matrix products, on_device(): exponent = jnp.exp(scores - row_peak)  7.73 us
  transfers between devices with their start and end apart: 3, of which 3 were waited for; matrix products, arithmetic and copies ran while one was open for 1% of the time, Pallas kernels for 0%

commit v1 on v0

--- a/solution.py
+++ b/solution.py
@@ -50,7 +50,9 @@
     partial_sum = jnp.einsum(
         "ltc,lcd->td", context, joining_weight, preferred_element_type=jnp.float32
     )
-    summed = lax.psum(partial_sum.astype(jnp.bfloat16), "tensor").astype(jnp.float32)
+    summed = jnp.sum(lax.all_gather(partial_sum.astype(jnp.bfloat16), "tensor"), axis=0).astype(
+        jnp.float32
+    )
     joined_rows = lax.dynamic_slice_in_dim(summed, offset, own_rows, 0)
     token_pos = offset + jnp.arange(own_rows, dtype=jnp.int32)
     chain_of = token_pos // seq_len

time: 237 us -> 269 us (1.14)
  waiting for transfers between devices: 143 us -> 164 us
  other arithmetic: 12.2 us -> 23.6 us
    all_gather x0 -> x1, waiting for transfers between devices: none -> 108 us  [on_device(): lax.all_gather(partial_sum.astype(jnp.bfloat16), 'tensor')]
    psum x1 -> x0, waiting for transfers between devices: 86.9 us -> none  [on_device(): lax.psum(partial_sum.astype(jnp.bfloat16), 'tensor').astype(jnp.float32)]
    reduce_sum x0 -> x1, other arithmetic: none -> 12 us  [on_device(): jnp.sum(lax.all_gather(partial_sum.astype(jnp.bfloat16), 'tensor'), axis=0)]
where the time goes in v1:
time: 269 us
  waiting for transfers between devices  164 us (61%)
  blocking collectives  39.8 us (15%)
  other arithmetic  23.6 us (9%)
  matrix products  19.5 us (7%)
  between operations  17.7 us (7%)
  local copies, waits for them, and re-layouts  4.04 us (2%)
    all_gather x1, waiting for transfers between devices, on_device(): lax.all_gather(partial_sum.astype(jnp.bfloat16), 'tensor')  108 us
    psum x1, blocking collectives, on_device(): lax.psum((local_gain, local_loss, jnp.sum(token_weight)), ('dp', 'tensor'))  39.8 us
    all_gather x1, waiting for transfers between devices, on_device(): lax.all_gather(grad_joined, 'tensor', axis=0, tiled=True)  34.6 us
    reduce_scatter x1, waiting for transfers between devices, on_device(): lax.psum_scatter(grad_total.astype(jnp.bfloat16), 'dp', scatter_dimension...  21.3 us
    reduce_sum x1, other arithmetic, on_device(): jnp.sum(lax.all_gather(partial_sum.astype(jnp.bfloat16), 'tensor'), axis=0)  12 us
    sub x1, matrix products, on_device(): exponent = jnp.exp(scores - row_peak)  7.73 us
  transfers between devices with their start and end apart: 3, of which 3 were waited for; matrix products, arithmetic and copies ran while one was open for 1% of the time, Pallas kernels for 0%

profile of v1, /device:TPU:0, one launch (start us, length us, event | category | flops | bytes accessed | tf_op | source)
XLA Modules:
  0.0 268.7 jit_solution(17279010306690435108)
XLA Ops:
  7.2 0.0 copy-start
  7.2 0.0 copy-start.2
  7.2 0.0 copy-start.3
  7.2 0.0 all-gather.6.cloned.1.call-start
  8.0 0.4 fusion.4
  8.4 2.0 reshape.122
  10.4 0.0 copy-done.2
  10.4 1.0 reshape.123
  11.4 0.0 copy-done.3
  11.4 1.0 copy.17
  12.4 7.7 %fusion.39 = (f32[2,1024]{1,0:T(2,128)S(1)}, f32[2,1024,1024]{1,2,0:T(8,128)}) fusion(pred[1024,1024]{0,1:T(8,128)(4,1)S(1)} %fusion.4, bf16[1024,2,128]{2,1,0:T(2,128)(2,1)} %reshape.123, bf16[1024,2,128]{2,1,0:T(2,128)(2,1)} %reshape.122), kind=kOutput, calls=%fused_computation.54 | convolution fusion | flops 545260544 | bytes 10493952 | tf_op jit(solution)/shard_map/sub | solution.py:39
  20.2 0.0 copy-done.4
  20.2 4.1 %fusion.20 = bf16[2,1024,128]{1,2,0:T(8,128)(2,1)S(1)} fusion(bf16[1024,2,128]{0,2,1:T(8,128)(2,1)S(1)} %bitcast.25, f32[2,1024,1024]{1,2,0:T(8,128)} %get-tuple-element.13, f32[2,1024]{1,0:T(2,128)S(1)} %get-tuple-element.12), kind=kOutput, calls=%fused_computation.29 | convolution fusion | flops 541327360 | bytes 9445376 | tf_op jit(solution)/shard_map/lchqk,lckhd->lcqhd/dot_general | solution.py:41
  24.3 0.0 copy-done
  24.3 3.2 %convolution_convert_fusion = bf16[1024,2048]{1,0:T(8,128)(2,1)} fusion(bf16[1024,256]{0,1:T(8,128)(2,1)S(1)} %bitcast.23, bf16[1,256,2048]{2,1,0:T(8,128)(2,1)S(1)} %copy-done), kind=kOutput, calls=%fused_computation.11 | convolution fusion | flops 1075838976 | bytes 5767168 | tf_op jit(solution)/shard_map/ltc,lcd->td/dot_general | solution.py:50
  27.5 0.0 all-gather.6.cloned.1.call-update
  27.5 0.0 all-gather.4.cloned.1.call-start
  28.2 108.1 %all-gather.6.cloned.1.call-done = bf16[4096,2048]{1,0:T(8,128)(2,1)} async-done(((bf16[1024,2048]{1,0:T(8,128)(2,1)}), bf16[4096,2048]{1,0:T(8,128)(2,1)}) %all-gather.6.cloned.1.call-update) | async-done | bytes 16777232 | tf_op jit(solution)/shard_map/all_gather | solution.py:53
  136.3 12.0 %reduce_sum.76 = bf16[1024,2048]{1,0:T(8,128)(2,1)} reduce(bf16[4,1024,2048]{2,1,0:T(8,128)(2,1)} %bitcast.22, bf16[]{:T(256)} %constant.49.clone.1), dimensions={0}, to_apply=%region_2.3 | reduce | flops 6291456 | bytes 20971522 | tf_op jit(solution)/shard_map/reduce_sum | solution.py:53
  148.3 1.5 fusion.19
  149.9 2.3 fusion.18
  152.2 3.4 %fusion.17 = (bf16[256,2048]{1,0:T(8,128)(2,1)}, bf16[256,2048]{1,0:T(8,128)(2,1)}) fusion(bf16[256,2048]{1,0:T(8,128)(2,1)S(1)} %copy-done.1, f32[256]{0:T(256)S(1)} %broadcast_multiply_fusion.1, f32[256]{0:T(256)S(1)} %broadcast_multiply_fusion, f32[2048]{0:T(1024)S(1)} %copy-done.5, f32[256]{0:T(256)S(1)} %add_rsqrt_fusion, ...), kind=kLoop, calls=%fused_computation.25 | loop fusion | flops 6291456 | bytes 4205572 | tf_op jit(solution)/shard_map/convert_element_type | solution.py:75
  155.6 0.0 all-gather.4.cloned.1.call-update
  155.6 0.0 reduce-scatter.2.cloned.1.call-start
  155.7 34.6 %all-gather.4.cloned.1.call-done = bf16[1024,2048]{1,0:T(8,128)(2,1)} async-done(((bf16[256,2048]{1,0:T(8,128)(2,1)}), bf16[1024,2048]{1,0:T(8,128)(2,1)}) %all-gather.4.cloned.1.call-update) | async-done | bytes 4194320 | tf_op jit(solution)/shard_map/all_gather | solution.py:82
  190.3 4.4 %fusion.11 = bf16[1,256,2048]{2,1,0:T(8,128)(2,1)} fusion(bf16[1024,256]{0,1:T(8,128)(2,1)S(1)} %bitcast.24, bf16[1024,2048]{1,0:T(8,128)(2,1)} %all-gather.4.cloned.1.call-done), kind=kOutput, calls=%fused_computation.19 | convolution fusion | flops 1074266112 | bytes 5767168 | tf_op jit(solution)/shard_map/ltc,td->lcd/dot_general | solution.py:79
  194.7 0.0 reduce-scatter.2.cloned.1.call-update
  194.7 0.7 multiply_reduce_fusion.1
  195.4 39.8 %all-reduce = (f32[]{:T(128)}, f32[2048]{0:T(1024)S(1)}, f32[]{:T(128)}) all-reduce(f32[]{:T(128)} %get-tuple-element.15, f32[2048]{0:T(1024)S(1)} %get-tuple-element.4, f32[]{:T(128)} %get-tuple-element.14), channel_id=1, replica_groups=mesh['dp'=8,'tensor'=4] {'dp','tensor'}, use_global_device_ids=true, to_apply=%region_7.8 | all-reduce | flops 2050 | bytes 16400 | tf_op jit(solution)/shard_map/psum | solution.py:76
  236.4 1.2 broadcast_divide_fusion
  237.6 21.3 %reduce-scatter.2.cloned.1.call-done = bf16[1,256,256]{2,1,0:T(8,128)(2,1)} async-done(((bf16[1,256,2048]{2,1,0:T(8,128)(2,1)}), bf16[1,256,256]{2,1,0:T(8,128)(2,1)}) %reduce-scatter.2.cloned.1.call-update) | async-done | bytes 131088 | tf_op jit(solution)/shard_map/reduce_scatter | solution.py:85
  258.9 2.1 divide_convert_fusion.4
  (9 shorter events, 0.0 us)
Async XLA Ops:
  7.2 17.1 %copy-start = (bf16[1,256,2048]{2,1,0:T(8,128)(2,1)S(1)}, bf16[1,256,2048]{2,1,0:T(8,128)(2,1)}, u32[]{:S(2)}) copy-start(bf16[1,256,2048]{2,1,0:T(8,128)(2,1)} %param.11) | copy-start | bytes 3145732
  7.2 3.3 %copy-start.2 = (bf16[1,1024,256]{2,1,0:T(8,128)(2,1)S(1)}, bf16[1,1024,256]{2,1,0:T(8,128)(2,1)}, u32[]{:S(2)}) copy-start(bf16[1,1024,256]{2,1,0:T(8,128)(2,1)} %param.9) | copy-start | bytes 1572868
  7.2 4.2 %copy-start.3 = (bf16[1,1024,256]{2,1,0:T(8,128)(2,1)S(1)}, bf16[1,1024,256]{2,1,0:T(8,128)(2,1)}, u32[]{:S(2)}) copy-start(bf16[1,1024,256]{2,1,0:T(8,128)(2,1)} %param.10) | copy-start | bytes 1572868
  7.2 129.1 %all-gather.6.cloned.1.call-start = ((), (), s32[]{:S(2)}) async-start(), calls=%async_computation.3 | async-start | bytes 20971520 | tf_op jit(solution)/shard_map/all_gather | solution.py:53
  12.4 7.7 %copy-start.4 = (bf16[1,1024,256]{1,2,0:T(8,128)(2,1)S(1)}, bf16[1,1024,256]{1,2,0:T(8,128)(2,1)}, u32[]{:S(2)}) copy-start(bf16[1,1024,256]{1,2,0:T(8,128)(2,1)} %copy.17) | copy-start | bytes 1572868
  27.5 162.7 %all-gather.4.cloned.1.call-start = ((), (), s32[]{:S(2)}) async-start(), calls=%async_computation.1 | async-start | bytes 5242880 | tf_op jit(solution)/shard_map/all_gather | solution.py:82
  136.3 13.5 %copy-start.1 = (bf16[256,2048]{1,0:T(8,128)(2,1)S(1)}, bf16[256,2048]{1,0:T(8,128)(2,1)}, u32[]{:S(2)}) copy-start(bf16[256,2048]{1,0:T(8,128)(2,1)} %param.13) | copy-start | bytes 3145732
  136.3 13.6 %copy-start.5 = (f32[2048]{0:T(1024)S(1)}, f32[2048]{0:T(1024)}, u32[]{:S(2)}) copy-start(f32[2048]{0:T(1024)} %param.12) | copy-start | bytes 24580
  155.6 103.2 %reduce-scatter.2.cloned.1.call-start = ((), (), s32[]{:S(2)}) async-start(), calls=%async_computation.2 | async-start | bytes 1179648 | tf_op jit(solution)/shard_map/reduce_scatter | solution.py:85
Sparse Core Ops, SparseCore 0:
  27.6 108.6 all-gather.5
  155.8 34.4 all-gather.3
  194.8 63.9 reduce-scatter.1
